TPU v7x, 32 devices: a whole 2x2x4 slice. The times are simulated.
32 devices in a mesh: groups: 2 (over y), feat: 4 (over z), layer: 2 (over x), row: 2 (over core).
Axes of the slice: x: 2, y: 2, z: 4, core: 2. Of those that a mesh axis runs over, the one named last changes fastest.
Arguments:
- resid_buf: bfloat16 [512, 2, 4608], P(('groups', 'feat', 'row')), parts along dimension 0, may hold values from -6 to 6
- shuffle: int32 [512], P('groups'), parts along dimension 0, may hold values from 0 to 255, each once
- mlp_out: bfloat16 [512, 2, 4608], P(('groups', 'feat', 'row')), parts along dimension 0, may hold values from -5 to 5
- enc_weight: bfloat16 [2, 8192, 4608], P('layer', 'feat', 'row'), may hold values from -0.09375 to 0.09375
- dec_weight: bfloat16 [2, 8192, 2, 4608], P('layer', 'feat', None, 'row'), may hold values from -0.0625 to 0.0625
- enc_bias: float32 [2, 8192], P('layer', 'feat'), may hold values from -0.5 to 0.5
- dec_bias: float32 [2, 4608], replicated, may hold values from -3 to 3
Outputs:
- rebuilt: bfloat16 [512, 2, 4608], P(('groups', 'feat', 'row')), parts along dimension 0
- enc_grad: bfloat16 [4, 8192, 4608], P(('groups', 'layer'), 'feat', 'row'), parts along dimension 0
- dec_grad: bfloat16 [4, 8192, 2, 4608], P(('groups', 'layer'), 'feat', None, 'row'), parts along dimension 0
- bias_grad: float32 [4, 8192], P(('groups', 'layer'), 'feat'), parts along dimension 0
There are 2 independent parts, one for each index of `groups`. A program takes and returns all parts, laid end to end along the dimension named above; an argument that names none is the same for every part. Nothing has to cross between parts.
Inputs may be any that keep to these rules, and one draw needn't show every extreme that they name: `shuffle`: a permutation of the 256 buffer rows.
All inputs are finite; a program needn't handle non-finite values.
Results may differ from a plain program's by a relative error of at most 0.04.
Values may be sent and summed in bfloat16 or wider, within the bound.
A program may use at most 128 MiB of HBM per device.

v0:
```python
import jax
import jax.numpy as jnp
from jax import lax
from jax.sharding import PartitionSpec as P

LAYERS = 2


def from_behind(block, axis, distance):
    devices = range(lax.axis_size(axis))
    route = [(i - distance, i) for i in devices if i - distance in devices]
    return lax.ppermute(block, axis, route)


def dot_last(left, right):
    return lax.dot_general(
        left, right, (((1,), (1,)), ((), ())), preferred_element_type=jnp.float32
    )


def dot_first(left, right):
    return lax.dot_general(
        left, right, (((0,), (0,)), ((), ())), preferred_element_type=jnp.float32
    )


def on_device(resid_buf, shuffle, mlp_out, enc_weight, dec_weight, enc_bias, dec_bias):
    feat_count = lax.axis_size("feat")
    row_count = lax.axis_size("row")
    sub_blocks = lax.axis_size("layer") // LAYERS
    layer_pos = lax.axis_index("layer")
    row_pos = lax.axis_index("row")
    source = layer_pos // sub_blocks
    rows_each = resid_buf.shape[0]
    width = dec_bias.shape[1]
    half_width = enc_weight.shape[2]
    local_rows = rows_each * feat_count
    total_rows = local_rows * row_count
    loss_scale = float(total_rows) ** (-0.5)
    own_layer = lax.dynamic_index_in_dim(resid_buf, source, axis=1, keepdims=False)
    buffer_all = lax.all_gather(own_layer, ("feat", "row"), axis=0, tiled=True)
    batch_rows = jnp.take(buffer_all, shuffle, axis=0)
    blocks = batch_rows.reshape(feat_count, row_count, rows_each, width)
    inputs_half = lax.dynamic_slice_in_dim(
        jnp.swapaxes(blocks, 0, 1), row_pos * half_width, half_width, axis=3
    )
    inputs_half = inputs_half.reshape(total_rows, half_width)
    own_half_dec = dec_weight[0][:, 0]
    next_half_dec = dec_weight[0][:, 1]
    pre_all = lax.psum(dot_last(inputs_half, enc_weight[0]), "row") + enc_bias[0]
    features_all = jnp.maximum(pre_all, 0.0).astype(jnp.bfloat16)
    own_part = jnp.dot(features_all, own_half_dec, preferred_element_type=jnp.float32)
    next_part = jnp.dot(features_all, next_half_dec, preferred_element_type=jnp.float32)
    carried = from_behind(next_part, "layer", sub_blocks)
    spread = (own_part + carried).reshape(row_count, local_rows, half_width)
    halves = lax.psum_scatter(spread, "feat", scatter_dimension=1, tiled=True)
    joined = lax.all_to_all(halves, "row", split_axis=0, concat_axis=2, tiled=True)
    section_sum = joined.reshape(rows_each, width)
    target_ids = jnp.arange(LAYERS, dtype=jnp.int32)
    target_slots = jnp.where((target_ids == source)[:, None, None], section_sum[None], 0.0)
    totals = lax.psum(target_slots, "layer")
    recon_sum = jnp.swapaxes(totals, 0, 1) + dec_bias[None]
    errors = (recon_sum - mlp_out.astype(jnp.float32)).astype(jnp.bfloat16)
    gathered = lax.all_gather(errors, ("feat", "row"), axis=0, tiled=True)
    error_grid = gathered.reshape(feat_count, row_count, rows_each, LAYERS, width)
    errors_mine = lax.dynamic_index_in_dim(error_grid, row_pos, axis=1, keepdims=False)
    errors_mine = errors_mine.reshape(local_rows, LAYERS, width)
    errors_half = lax.dynamic_slice_in_dim(
        jnp.swapaxes(error_grid, 0, 1), row_pos * half_width, half_width, axis=4
    )
    errors_half = errors_half.reshape(total_rows, LAYERS, half_width)
    live_next = source + 1 < LAYERS
    next_index = jnp.minimum(source + 1, LAYERS - 1)
    half_own = lax.dynamic_index_in_dim(errors_half, source, axis=1, keepdims=False)
    half_next = lax.dynamic_index_in_dim(errors_half, next_index, axis=1, keepdims=False)
    half_next = jnp.where(live_next, half_next, jnp.zeros_like(half_next))
    half_terms = dot_last(half_own, own_half_dec) + dot_last(half_next, next_half_dec)
    grad_feats = lax.psum(half_terms, "row") * loss_scale
    grad_all = jnp.where(pre_all > 0, grad_feats, 0.0).astype(jnp.bfloat16)
    grad_own = loss_scale * dot_first(features_all, half_own)
    grad_next = loss_scale * dot_first(features_all, half_next)
    enc_grad = dot_first(grad_all, inputs_half).astype(jnp.bfloat16)
    dec_grad = jnp.stack([grad_own, grad_next], axis=1).astype(jnp.bfloat16)
    bias_grad = jnp.sum(grad_all.astype(jnp.float32), axis=0)
    return (recon_sum.astype(jnp.bfloat16), enc_grad[None], dec_grad[None], bias_grad[None])


def solution(mesh):
    return jax.shard_map(
        on_device,
        mesh=mesh,
        in_specs=(
            P(("groups", "feat", "row"), None, None),
            P("groups"),
            P(("groups", "feat", "row"), None, None),
            P("layer", "feat", "row"),
            P("layer", "feat", None, "row"),
            P("layer", "feat"),
            P(),
        ),
        out_specs=(
            P(("groups", "feat", "row"), None, None),
            P(("groups", "layer"), "feat", "row"),
            P(("groups", "layer"), "feat", None, "row"),
            P(("groups", "layer"), "feat"),
        ),
        check_vma=False,
    )
```

profile of v0, /device:TPU:0, one launch (start us, length us, event | category | flops | bytes accessed | tf_op | source)
XLA Modules:
  0.0 529.7 jit_solution(15762774988231695739)
XLA Ops:
  9.8 34.6 %all-gather.6.cloned.1.call-done = bf16[256,1,4608]{2,0,1:T(8,128)(2,1)} async-done(((bf16[32,1,4608]{2,0,1:T(8,128)(2,1)}), bf16[256,1,4608]{2,0,1:T(8,128)(2,1)}) %all-gather.6.cloned.1.call-update) | async-done | bytes 2359312 | tf_op jit(solution)/shard_map/all_gather | solution.py:41
  44.4 6.3 %gather_fusion = bf16[256,4608]{1,0:T(8,128)(2,1)S(1)} fusion(bf16[256,4608]{1,0:T(8,128)(2,1)} %bitcast.65, s32[1024]{0:T(1024)S(1)} %pad_clamp_fusion), kind=kCustom, calls=%fused_computation | custom fusion | bytes 4719616 | tf_op jit(solution)/shard_map/jit(_take)/gather | solution.py:42
  52.0 7.6 %fusion.3 = f32[256,2048]{1,0:T(8,128)} fusion(bf16[256,2304]{1,0:T(8,128)(2,1)S(1)} %bitcast.71, bf16[1,2048,2304]{2,1,0:T(8,128)(2,1)} %param.10), kind=kOutput, calls=%fused_computation.11 | convolution fusion | flops 2415919104 | bytes 12713984 | tf_op jit(solution)/shard_map/dot_general | solution.py:16
  59.7 18.2 %copy.45 = bf16[1,2048,2,2304]{3,1,2,0:T(8,128)(2,1)} copy(bf16[1,2048,2,2304]{3,2,1,0:T(2,128)(2,1)} %param.11) | data formatting | bytes 37748736 | tf_op args[4]
  77.9 2.4 all-reduce.6.cloned.1.call-done
  80.4 2.0 maximum_convert_fusion
  82.3 6.6 %fusion.8 = f32[256,2304]{1,0:T(8,128)S(1)} fusion(bf16[256,2048]{1,0:T(8,128)(2,1)S(1)} %maximum_convert_fusion, bf16[2048,2,2304]{2,0,1:T(8,128)(2,1)} %bitcast.66), kind=kOutput, calls=%fused_computation.16 | convolution fusion | flops 2415919104 | bytes 12845056 | tf_op jit(solution)/shard_map/dot_general | solution.py:53
  89.0 4.1 collective-permute-start
  93.1 50.6 %collective-permute-done = f32[256,2304]{1,0:T(8,128)S(1)} collective-permute-done((f32[256,2304]{1,0:T(8,128)S(1)}, f32[256,2304]{1,0:T(8,128)S(1)}, u32[]{:S(2)}, u32[]{:S(2)}) %collective-permute-start) | collective-permute-done | bytes 2359328 | tf_op jit(solution)/shard_map/ppermute | solution.py:12
  143.7 2.7 fusion.9
  146.4 3.2 copy.32
  151.5 94.8 %all-reduce.12.cloned.1.call-done = f32[2,128,2304]{2,0,1:T(2,128)} async-done(((f32[2,128,2304]{2,0,1:T(2,128)}), f32[2,128,2304]{2,0,1:T(2,128)}) %all-reduce.12.cloned.1.call-update) | async-done | bytes 2359312
  247.5 4.2 all_to_all.15
  253.5 42.1 %all-reduce.8.cloned.1.call-done = f32[2,32,4608]{2,1,0:T(8,128)} async-done(((f32[2,32,4608]{2,1,0:T(8,128)}), f32[2,32,4608]{2,1,0:T(8,128)}) %all-reduce.8.cloned.1.call-update) | async-done | bytes 1179664 | tf_op jit(solution)/shard_map/psum | solution.py:61
  295.6 2.5 fusion.15
  299.7 49.8 %all-gather.4.cloned.1.call-done = bf16[256,2,4608]{2,0,1:T(8,128)(2,1)} async-done(((bf16[32,2,4608]{2,0,1:T(8,128)(2,1)}), bf16[256,2,4608]{2,0,1:T(8,128)(2,1)}) %all-gather.4.cloned.1.call-update) | async-done | bytes 4718608 | tf_op jit(solution)/shard_map/all_gather | solution.py:64
  351.5 6.1 %fusion.5 = f32[256,2048]{1,0:T(8,128)S(1)} fusion(bf16[2048,2,2304]{2,0,1:T(8,128)(2,1)} %bitcast.67, bf16[256,2,2304]{2,0,1:T(8,128)(2,1)S(1)} %bitcast.73, s32[]{:T(128)S(6)} %select_n.47), kind=kOutput, calls=%fused_computation.13 | convolution fusion | flops 2415919104 | bytes 12713988 | tf_op jit(solution)/shard_map/dot_general | solution.py:16
  357.6 7.7 %fusion.10 = f32[256,2048]{1,0:T(8,128)} fusion(f32[256,2048]{1,0:T(8,128)S(1)} %fusion.5, bf16[2048,2,2304]{2,0,1:T(8,128)(2,1)} %bitcast.68, bf16[256,2,2304]{2,0,1:T(8,128)(2,1)S(1)} %bitcast.74, s32[]{:T(128)S(6)} %select_n.52, pred[]{:T(512)S(6)} %lt.28), kind=kOutput, calls=%fused_computation.18 | convolution fusion | flops 2417033216 | bytes 14811141 | tf_op jit(solution)/shard_map/dot_general | solution.py:16
  365.3 4.4 fusion.1
  369.7 5.2 fusion.2
  374.9 7.4 %pad_maximum_fusion = bf16[1,2048,2,2304]{3,1,2,0:T(8,128)(2,1)S(1)} fusion(bf16[1,2048,1,2304]{3,1,2,0:T(8,128)(2,1)} %fusion.2, bf16[1,2048,1,2304]{3,1,2,0:T(8,128)(2,1)S(1)} %fusion.1), kind=kLoop, calls=%fused_computation.1 | loop fusion | flops 9437184 | bytes 37748736 | tf_op jit(solution)/shard_map/stack | solution.py:83
  382.3 132.7 %copy.38 = bf16[1,2048,2,2304]{3,2,1,0:T(2,128)(2,1)} copy(bf16[1,2048,2,2304]{3,1,2,0:T(8,128)(2,1)S(1)} %pad_maximum_fusion) | data formatting | bytes 37748736
  515.0 2.7 convert_reduce_fusion
  517.7 5.2 fusion
  (58 shorter events, 11.7 us)
Async XLA Ops:
  7.2 1.1 copy-start
  7.2 2.5 copy-start.11
  7.2 37.2 %all-gather.6.cloned.1.call-start = ((), (), s32[]{:S(2)}) async-start(), calls=%async_computation.5 | async-start | bytes 2654208 | tf_op jit(solution)/shard_map/all_gather | solution.py:41
  9.6 70.7 %all-reduce.6.cloned.1.call-start = ((), (), s32[]{:S(2)}) async-start(), calls=%async_computation.1 | async-start | bytes 4194304 | tf_op jit(solution)/shard_map/psum | solution.py:50
  51.0 1.0 copy-start.4
  59.7 20.7 %copy-start.10 = (f32[1,2048]{1,0:T(1,128)S(1)}, f32[1,2048]{1,0:T(1,128)}, u32[]{:S(2)}) copy-start(f32[1,2048]{1,0:T(1,128)} %param.12) | copy-start | bytes 24580
  59.7 186.7 %all-reduce.12.cloned.1.call-start = ((), (), s32[]{:S(2)}) async-start(), calls=%async_computation.6 | async-start | bytes 4718592
  80.4 63.3 %copy-start.2 = (bf16[1,2048,2,2304]{3,1,2,0:T(8,128)(2,1)S(1)}, bf16[1,2048,2,2304]{3,1,2,0:T(8,128)(2,1)}, u32[]{:S(2)}) copy-start(bf16[1,2048,2,2304]{3,1,2,0:T(8,128)(2,1)} %copy.45) | copy-start | bytes 56623108
  89.0 54.7 %collective-permute-start = (f32[256,2304]{1,0:T(8,128)S(1)}, f32[256,2304]{1,0:T(8,128)S(1)}, u32[]{:S(2)}, u32[]{:S(2)}) collective-permute-start(f32[256,2304]{1,0:T(8,128)S(1)} %fusion.8), channel_id=1, source_target_pairs={{0,2},{1,3},{4,6},{5,7},{8,10},{9,11},{12,14},{13,15},{16,18},{17,... | collective-permute-start | bytes 7077896 | tf_op jit(solution)/shard_map/ppermute | solution.py:12
  149.6 0.7 copy-start.12
  149.7 145.9 %all-reduce.8.cloned.1.call-start = ((), (), s32[]{:S(2)}) async-start(), calls=%async_computation.2 | async-start | bytes 2359296 | tf_op jit(solution)/shard_map/psum | solution.py:61
  252.2 43.4 %copy-start.9 = (f32[2,4608]{1,0:T(2,128)S(1)}, f32[2,4608]{1,0:T(2,128)}, u32[]{:S(2)}) copy-start(f32[2,4608]{1,0:T(2,128)} %param.13) | copy-start | bytes 110596
  253.4 96.0 %all-gather.4.cloned.1.call-start = ((), (), s32[]{:S(2)}) async-start(), calls=%async_computation.3 | async-start | bytes 5308416 | tf_op jit(solution)/shard_map/all_gather | solution.py:64
  295.6 2.6 copy-start.6
  298.1 216.9 %all-reduce.10.cloned.1.call-start = ((), (), s32[]{:S(2)}) async-start(), calls=%async_computation.4 | async-start | bytes 4194304 | tf_op jit(solution)/shard_map/psum | solution.py:78
  351.5 6.1 %copy-start.7 = (bf16[2,4,32,2,2304]{4,2,1,0,3:T(8,128)(2,1)}, bf16[2,4,32,2,2304]{4,2,1,0,3:T(8,128)(2,1)S(1)}, u32[]{:S(2)}) copy-start(bf16[2,4,32,2,2304]{4,2,1,0,3:T(8,128)(2,1)S(1)} %copy.36) | copy-start | bytes 7077892
  365.3 4.4 copy-start.8
  382.3 132.7 %copy-start.3 = (f32[256,2048]{1,0:T(8,128)S(1)}, f32[256,2048]{1,0:T(8,128)}, u32[]{:S(2)}) copy-start(f32[256,2048]{1,0:T(8,128)} %all-reduce.6.cloned.1.call-done) | copy-start | bytes 6291460
  515.0 2.7 copy-start.5
  517.7 5.2 copy-start.1
Sparse Core Ops, SparseCore 0:
  10.2 34.1 all-gather.5
  59.8 20.5 all-reduce.5
  149.8 96.5 all-reduce.11
  253.6 41.9 all-reduce.7
  298.2 51.1 all-gather.3
  365.4 20.0 all-reduce.9
where the time goes:
time: 530 us
  waiting for transfers between devices  274 us (52%)
  local copies, waits for them, and re-layouts  170 us (32%)
  matrix products  45.5 us (9%)
  other arithmetic  16.1 us (3%)
  between operations  15 us (3%)
    unnamed x33, local copies, waits for them, and re-layouts  157 us
    unnamed x7, waiting for transfers between devices  94.9 us
    ppermute x1, waiting for transfers between devices, from_behind(): return lax.ppermute(block, axis, route)  50.6 us
    all_gather x1, waiting for transfers between devices, on_device(): gathered = lax.all_gather(errors, ('feat', 'row'), axis=0, tiled=True)  49.8 us
    psum x1, waiting for transfers between devices, on_device(): totals = lax.psum(target_slots, 'layer')  42.1 us
    all_gather x1, waiting for transfers between devices, on_device(): buffer_all = lax.all_gather(own_layer, ('feat', 'row'), axis=0, tiled=True)  34.6 us
    dot_general x3, matrix products, dot_last(): lax.dot_general(left, right, (((1,), (1,)), ((), ())), preferred_element_...  21.3 us
    dot_general x3, matrix products, dot_first(): lax.dot_general(left, right, (((0,), (0,)), ((), ())), preferred_element_...  14.8 us
  transfers between devices with their start and end apart: 7, of which 6 were waited for; matrix products, arithmetic and copies ran while one was open for 32% of the time, Pallas kernels for 0%

commit v1 on v0

--- a/solution.py
+++ b/solution.py
@@ -58,7 +58,7 @@
     section_sum = joined.reshape(rows_each, width)
     target_ids = jnp.arange(LAYERS, dtype=jnp.int32)
     target_slots = jnp.where((target_ids == source)[:, None, None], section_sum[None], 0.0)
-    totals = lax.psum(target_slots, "layer")
+    totals = jnp.sum(lax.all_gather(target_slots, "layer"), axis=0)
     recon_sum = jnp.swapaxes(totals, 0, 1) + dec_bias[None]
     errors = (recon_sum - mlp_out.astype(jnp.float32)).astype(jnp.bfloat16)
     gathered = lax.all_gather(errors, ("feat", "row"), axis=0, tiled=True)

time: 530 us -> 524 us (0.989)
  waiting for transfers between devices: 274 us -> 268 us
    psum x1 -> x0, waiting for transfers between devices: 42.1 us -> none  [on_device(): totals = lax.psum(target_slots, 'layer')]
    all_gather x0 -> x1, waiting for transfers between devices: none -> 35.2 us  [on_device(): totals = jnp.sum(lax.all_gather(target_slots, 'layer'), axis=0)]
  transfers between devices with their start and end apart: 7 -> 7, of which waited for: 6 -> 6; matrix products, arithmetic and copies ran while one was open for 32% -> 33% of each run, Pallas kernels for 0% -> 0%
where the time goes in v1:
time: 524 us; the launch traced here: 523 us
  waiting for transfers between devices  268 us (51%)
  local copies, waits for them, and re-layouts  170 us (32%)
  matrix products  45.4 us (9%)
  other arithmetic  16.5 us (3%)
  between operations  15 us (3%)
    unnamed x33, local copies, waits for them, and re-layouts  157 us
    unnamed x7, waiting for transfers between devices  94.9 us
    ppermute x1, waiting for transfers between devices, from_behind(): return lax.ppermute(block, axis, route)  50.6 us
    all_gather x1, waiting for transfers between devices, on_device(): gathered = lax.all_gather(errors, ('feat', 'row'), axis=0, tiled=True)  49.8 us
    all_gather x1, waiting for transfers between devices, on_device(): totals = jnp.sum(lax.all_gather(target_slots, 'layer'), axis=0)  35.2 us
    all_gather x1, waiting for transfers between devices, on_device(): buffer_all = lax.all_gather(own_layer, ('feat', 'row'), axis=0, tiled=True)  34.6 us
    dot_general x3, matrix products, dot_last(): lax.dot_general(left, right, (((1,), (1,)), ((), ())), preferred_element_...  21.3 us
    dot_general x3, matrix products, dot_first(): lax.dot_general(left, right, (((0,), (0,)), ((), ())), preferred_element_...  14.8 us
  transfers between devices with their start and end apart: 7, of which 6 were waited for; matrix products, arithmetic and copies ran while one was open for 33% of the time, Pallas kernels for 0%

profile of v1, /device:TPU:0, one launch (start us, length us, event | category | flops | bytes accessed | tf_op | source)
XLA Modules:
  0.0 523.2 jit_solution(17151724039423448602)
XLA Ops:
  9.8 34.6 %all-gather.9.cloned.1.call-done = bf16[256,1,4608]{2,0,1:T(8,128)(2,1)} async-done(((bf16[32,1,4608]{2,0,1:T(8,128)(2,1)}), bf16[256,1,4608]{2,0,1:T(8,128)(2,1)}) %all-gather.9.cloned.1.call-update) | async-done | bytes 2359312 | tf_op jit(solution)/shard_map/all_gather | solution.py:41
  44.4 6.3 %gather_fusion = bf16[256,4608]{1,0:T(8,128)(2,1)S(1)} fusion(bf16[256,4608]{1,0:T(8,128)(2,1)} %bitcast.65, s32[1024]{0:T(1024)S(1)} %pad_clamp_fusion), kind=kCustom, calls=%fused_computation | custom fusion | bytes 4719616 | tf_op jit(solution)/shard_map/jit(_take)/gather | solution.py:42
  52.0 7.6 %fusion.3 = f32[256,2048]{1,0:T(8,128)} fusion(bf16[256,2304]{1,0:T(8,128)(2,1)S(1)} %bitcast.71, bf16[1,2048,2304]{2,1,0:T(8,128)(2,1)} %param.10), kind=kOutput, calls=%fused_computation.11 | convolution fusion | flops 2415919104 | bytes 12713984 | tf_op jit(solution)/shard_map/dot_general | solution.py:16
  59.7 18.2 %copy.45 = bf16[1,2048,2,2304]{3,1,2,0:T(8,128)(2,1)} copy(bf16[1,2048,2,2304]{3,2,1,0:T(2,128)(2,1)} %param.11) | data formatting | bytes 37748736 | tf_op args[4]
  77.9 2.4 all-reduce.5.cloned.1.call-done
  80.4 2.0 maximum_convert_fusion
  82.3 6.6 %fusion.8 = f32[256,2304]{1,0:T(8,128)S(1)} fusion(bf16[256,2048]{1,0:T(8,128)(2,1)S(1)} %maximum_convert_fusion, bf16[2048,2,2304]{2,0,1:T(8,128)(2,1)} %bitcast.66), kind=kOutput, calls=%fused_computation.16 | convolution fusion | flops 2415919104 | bytes 12845056 | tf_op jit(solution)/shard_map/dot_general | solution.py:53
  89.0 4.1 collective-permute-start
  93.1 50.6 %collective-permute-done = f32[256,2304]{1,0:T(8,128)S(1)} collective-permute-done((f32[256,2304]{1,0:T(8,128)S(1)}, f32[256,2304]{1,0:T(8,128)S(1)}, u32[]{:S(2)}, u32[]{:S(2)}) %collective-permute-start) | collective-permute-done | bytes 2359328 | tf_op jit(solution)/shard_map/ppermute | solution.py:12
  143.7 2.7 fusion.9
  146.4 3.2 copy.32
  151.5 94.8 %all-reduce.9.cloned.1.call-done = f32[2,128,2304]{2,0,1:T(2,128)} async-done(((f32[2,128,2304]{2,0,1:T(2,128)}), f32[2,128,2304]{2,0,1:T(2,128)}) %all-reduce.9.cloned.1.call-update) | async-done | bytes 2359312
  247.5 4.2 all_to_all.15
  253.5 35.2 %all-gather.5.cloned.1.call-done = f32[2,2,32,4608]{3,2,1,0:T(8,128)} async-done(((f32[1,2,32,4608]{3,2,1,0:T(8,128)}), f32[2,2,32,4608]{3,2,1,0:T(8,128)}) %all-gather.5.cloned.1.call-update) | async-done | bytes 2359312 | tf_op jit(solution)/shard_map/all_gather | solution.py:61
  288.7 1.9 reduce_sum.18
  293.2 49.8 %all-gather.7.cloned.1.call-done = bf16[256,2,4608]{2,0,1:T(8,128)(2,1)} async-done(((bf16[32,2,4608]{2,0,1:T(8,128)(2,1)}), bf16[256,2,4608]{2,0,1:T(8,128)(2,1)}) %all-gather.7.cloned.1.call-update) | async-done | bytes 4718608 | tf_op jit(solution)/shard_map/all_gather | solution.py:64
  345.0 6.0 %fusion.5 = f32[256,2048]{1,0:T(8,128)S(1)} fusion(bf16[2048,2,2304]{2,0,1:T(8,128)(2,1)} %bitcast.67, bf16[256,2,2304]{2,0,1:T(8,128)(2,1)S(1)} %bitcast.73, s32[]{:T(128)S(6)} %select_n.54), kind=kOutput, calls=%fused_computation.13 | convolution fusion | flops 2415919104 | bytes 12713988 | tf_op jit(solution)/shard_map/dot_general | solution.py:16
  351.1 7.7 %fusion.10 = f32[256,2048]{1,0:T(8,128)} fusion(f32[256,2048]{1,0:T(8,128)S(1)} %fusion.5, bf16[2048,2,2304]{2,0,1:T(8,128)(2,1)} %bitcast.68, bf16[256,2,2304]{2,0,1:T(8,128)(2,1)S(1)} %bitcast.74, s32[]{:T(128)S(6)} %select_n.59, pred[]{:T(512)S(6)} %lt.28), kind=kOutput, calls=%fused_computation.18 | convolution fusion | flops 2417033216 | bytes 14811141 | tf_op jit(solution)/shard_map/dot_general | solution.py:16
  358.8 4.4 fusion.1
  363.2 5.2 fusion.2
  368.4 7.4 %pad_maximum_fusion = bf16[1,2048,2,2304]{3,1,2,0:T(8,128)(2,1)S(1)} fusion(bf16[1,2048,1,2304]{3,1,2,0:T(8,128)(2,1)} %fusion.2, bf16[1,2048,1,2304]{3,1,2,0:T(8,128)(2,1)S(1)} %fusion.1), kind=kLoop, calls=%fused_computation.1 | loop fusion | flops 9437184 | bytes 37748736 | tf_op jit(solution)/shard_map/stack | solution.py:83
  375.8 132.7 %copy.38 = bf16[1,2048,2,2304]{3,2,1,0:T(2,128)(2,1)} copy(bf16[1,2048,2,2304]{3,1,2,0:T(8,128)(2,1)S(1)} %pad_maximum_fusion) | data formatting | bytes 37748736
  508.5 2.7 convert_reduce_fusion
  511.2 5.2 fusion
  (59 shorter events, 12.6 us)
Async XLA Ops:
  7.2 1.1 copy-start
  7.2 2.5 copy-start.11
  7.2 37.2 %all-gather.9.cloned.1.call-start = ((), (), s32[]{:S(2)}) async-start(), calls=%async_computation.5 | async-start | bytes 2654208 | tf_op jit(solution)/shard_map/all_gather | solution.py:41
  9.6 70.7 %all-reduce.5.cloned.1.call-start = ((), (), s32[]{:S(2)}) async-start(), calls=%async_computation.1 | async-start | bytes 4194304 | tf_op jit(solution)/shard_map/psum | solution.py:50
  51.0 1.0 copy-start.4
  59.7 20.7 %copy-start.10 = (f32[1,2048]{1,0:T(1,128)S(1)}, f32[1,2048]{1,0:T(1,128)}, u32[]{:S(2)}) copy-start(f32[1,2048]{1,0:T(1,128)} %param.12) | copy-start | bytes 24580
  59.7 186.7 %all-reduce.9.cloned.1.call-start = ((), (), s32[]{:S(2)}) async-start(), calls=%async_computation.6 | async-start | bytes 4718592
  80.4 63.3 %copy-start.2 = (bf16[1,2048,2,2304]{3,1,2,0:T(8,128)(2,1)S(1)}, bf16[1,2048,2,2304]{3,1,2,0:T(8,128)(2,1)}, u32[]{:S(2)}) copy-start(bf16[1,2048,2,2304]{3,1,2,0:T(8,128)(2,1)} %copy.45) | copy-start | bytes 56623108
  89.0 54.7 %collective-permute-start = (f32[256,2304]{1,0:T(8,128)S(1)}, f32[256,2304]{1,0:T(8,128)S(1)}, u32[]{:S(2)}, u32[]{:S(2)}) collective-permute-start(f32[256,2304]{1,0:T(8,128)S(1)} %fusion.8), channel_id=1, source_target_pairs={{0,2},{1,3},{4,6},{5,7},{8,10},{9,11},{12,14},{13,15},{16,18},{17,... | collective-permute-start | bytes 7077896 | tf_op jit(solution)/shard_map/ppermute | solution.py:12
  149.6 0.7 copy-start.12
  149.7 139.0 %all-gather.5.cloned.1.call-start = ((), (), s32[]{:S(2)}) async-start(), calls=%async_computation.2 | async-start | bytes 3538944 | tf_op jit(solution)/shard_map/all_gather | solution.py:61
  253.4 37.2 %copy-start.8 = (bf16[32,2,4608]{2,1,0:T(2,128)(2,1)S(1)}, bf16[32,2,4608]{2,1,0:T(2,128)(2,1)}, u32[]{:S(2)}) copy-start(bf16[32,2,4608]{2,1,0:T(2,128)(2,1)} %param.9) | copy-start | bytes 1769476
  253.4 37.2 %copy-start.9 = (f32[2,4608]{1,0:T(2,128)S(1)}, f32[2,4608]{1,0:T(2,128)}, u32[]{:S(2)}) copy-start(f32[2,4608]{1,0:T(2,128)} %param.13) | copy-start | bytes 110596
  253.4 89.5 %all-gather.7.cloned.1.call-start = ((), (), s32[]{:S(2)}) async-start(), calls=%async_computation.3 | async-start | bytes 5308416 | tf_op jit(solution)/shard_map/all_gather | solution.py:64
  291.6 216.9 %all-reduce.7.cloned.1.call-start = ((), (), s32[]{:S(2)}) async-start(), calls=%async_computation.4 | async-start | bytes 4194304 | tf_op jit(solution)/shard_map/psum | solution.py:78
  345.0 6.1 %copy-start.6 = (bf16[2,4,32,2,2304]{4,2,1,0,3:T(8,128)(2,1)}, bf16[2,4,32,2,2304]{4,2,1,0,3:T(8,128)(2,1)S(1)}, u32[]{:S(2)}) copy-start(bf16[2,4,32,2,2304]{4,2,1,0,3:T(8,128)(2,1)S(1)} %copy.36) | copy-start | bytes 7077892
  358.8 4.4 copy-start.7
  375.8 132.7 %copy-start.3 = (f32[256,2048]{1,0:T(8,128)S(1)}, f32[256,2048]{1,0:T(8,128)}, u32[]{:S(2)}) copy-start(f32[256,2048]{1,0:T(8,128)} %all-reduce.5.cloned.1.call-done) | copy-start | bytes 6291460
  508.5 2.7 copy-start.5
  511.2 5.2 copy-start.1
Sparse Core Ops, SparseCore 0:
  10.2 34.1 all-gather.8
  59.8 20.5 all-reduce.4
  149.8 96.5 all-reduce.8
  253.6 35.0 all-gather.4
  291.7 51.1 all-gather.6
  358.9 20.0 all-reduce.6
